TPU v7x, 32 devices: a whole 2x2x4 slice. The times are simulated.
32 devices in a mesh: ctx: 8 (over y, x, core), ch: 4 (over z).
Axes of the slice: x: 2, y: 2, z: 4, core: 2. Of those that a mesh axis runs over, the one named last changes fastest.
Arguments:
- q_short: bfloat16 [1024, 8192], P('ctx', 'ch'), may hold values from -6 to 6
- k_short: bfloat16 [1024, 8192], P('ctx', 'ch'), may hold values from -6 to 6
- v_input: bfloat16 [1024, 8192], P('ctx', 'ch'), may hold values from -6 to 6
- q_long: bfloat16 [1024, 8192], P('ctx', 'ch'), may hold values from -6 to 6
- k_long: bfloat16 [1024, 8192], P('ctx', 'ch'), may hold values from -6 to 6
- short_filter: bfloat16 [128, 512], P(None, 'ch'), may hold values from -0.5 to 0.5
- decay_rates: float32 [512, 16], P('ch'), may hold values from 0.0001953125 to 0.04
- residues: float32 [512, 16], P('ch'), may hold values from -1.5 to 1.5
Outputs:
- mixed: bfloat16 [1024, 8192], P('ctx', 'ch')
All inputs are finite; a program needn't handle non-finite values.
Results may differ from a plain program's by a relative error of at most 0.0065.
Values may be sent and summed in bfloat16 or wider, within the bound.
A program may use at most 64 MiB of HBM per device.

v0:
```python
import functools

import jax
import jax.numpy as jnp
from jax import lax
from jax.experimental import pallas as pl
from jax.experimental.pallas import tpu as pltpu
from jax.sharding import PartitionSpec as P

MESH = pl.DeviceIdType.MESH
LANES = 128
F32 = jnp.float32
BF16 = jnp.bfloat16


def iota(shape, dim):
    return lax.broadcasted_iota(jnp.int32, shape, dim)


def split(x):
    hi = x.astype(BF16)
    return hi, (x - hi.astype(F32)).astype(BF16)


def kernel(
    n, chunks, q_short_in, k_short_in, v_input_in, q_long_in, k_long_in, taps, rates, weights, out,
    q_short, q_long, k_long, k_short, v_input, fetch_sem,
    ubuf, ulong, ynear, short_tab, long_tab, in_tab, out_tab, lam_rc, short_row, long_row, modes,
    state, psend, precv, halo_send, halo_recv, scan_send, scan_recv,
):
    me = lax.axis_index("ctx")
    tokens, ch = k_short_in.shape
    half = tokens // 2
    order, groups = rates.shape
    share = ch // groups
    per = LANES // share
    blocks = ch // LANES
    per_chunk = blocks // chunks
    width = per_chunk * LANES
    levels = n.bit_length() - 1

    barrier = pltpu.get_barrier_semaphore()
    for step in range(1, n):
        pl.semaphore_signal(
            barrier, inc=1, device_id={"ctx": lax.rem(me + step, n)}, device_id_type=MESH
        )

    fetches = [
        pltpu.make_async_copy(source, target, fetch_sem.at[i])
        for i, (source, target) in enumerate(
            (
                (q_short_in, q_short),
                (k_long_in, k_long),
                (q_long_in, q_long),
                (k_short_in, k_short),
                (v_input_in, v_input),
            )
        )
    ]
    for i in (3, 4):
        fetches[i].start()
    fetches[3].wait()
    fetches[4].wait()
    for i in (0, 1, 2):
        fetches[i].start()

    ubuf[pl.ds(tokens, tokens), :] = (k_short[...].astype(F32) * v_input[...].astype(F32)).astype(BF16)

    pl.semaphore_wait(barrier, n - 1)

    def halo(c):
        cols = pl.ds(c * width, width)
        return pltpu.make_async_remote_copy(
            src_ref=ubuf.at[pl.ds(tokens, tokens), cols],
            dst_ref=ubuf.at[pl.ds(0, tokens), cols],
            send_sem=halo_send.at[c],
            recv_sem=halo_recv.at[c],
            device_id={"ctx": lax.rem(me + 1, n)},
            device_id_type=MESH,
        )

    @pl.when(me < n - 1)
    def _():
        for c in range(chunks):
            halo(c).start()

    @pl.when(me == 0)
    def _():
        ubuf[pl.ds(0, tokens), :] = jnp.zeros((tokens, ch), BF16)

    ubuf[pl.ds(2 * tokens, half), :] = jnp.zeros((half, ch), BF16)
    ulong[pl.ds(0, half), :] = jnp.zeros((half, ch), BF16)

    rate = jnp.transpose(rates[...])
    scaled = jnp.transpose(weights[...]) * jnp.sqrt(2.0 * rate)
    reverse = lax.rem(tokens - iota((1, tokens), 1), tokens).astype(F32)
    total = jnp.zeros((groups, tokens), F32)
    for r in range(order):
        total = total + scaled[:, r : r + 1] * jnp.exp(-rate[:, r : r + 1] * reverse)
    long_row[...] = total
    flip = (lax.rem(iota((tokens, tokens), 0) + iota((tokens, tokens), 1), tokens) == 0).astype(BF16)
    taps_t = jnp.transpose(taps[...].astype(F32)).astype(BF16)
    short_row[...] = jnp.dot(taps_t, flip, preferred_element_type=F32)

    spread = (lax.rem(iota((order, LANES), 1), order) == iota((order, LANES), 0)).astype(F32)
    own = lax.rem(iota((groups, LANES), 0), per) == iota((groups, LANES), 1) // order

    def row_modes(x):
        wide = jnp.dot(x, spread, precision=lax.Precision.HIGHEST, preferred_element_type=F32)
        return jnp.where(own, wide, 0.0)

    rate_wide = row_modes(rate)
    modes[0] = jnp.sum(rate_wide.reshape(blocks, per, LANES), axis=1)
    modes[1] = jnp.sum(row_modes(scaled).reshape(blocks, per, LANES), axis=1)
    rate_tall = jnp.transpose(rate_wide)

    diag = iota((LANES, LANES), 0) // order == iota((LANES, LANES), 1) // share
    rows_half = iota((half, tokens), 0)
    lower = rows_half >= iota((half, tokens), 1)
    causal = rows_half + half >= iota((half, tokens), 1)

    def compact(x):
        return jnp.sum(jnp.where(diag, x, 0.0).reshape(per, order, LANES), axis=0)

    for b in range(blocks):
        in_block = iota((LANES, groups), 1) // per == b
        column = jnp.sum(jnp.where(in_block, rate_tall, 0.0), axis=1, keepdims=True)
        lam_rc[:, pl.ds(b * LANES, LANES)] = compact(jnp.broadcast_to(column, (LANES, LANES)))
        ahead = (tokens - iota((LANES, tokens), 1)).astype(F32)
        hi, lo = split(jnp.exp(-column * ahead))
        in_tab[b, :, pl.ds(0, tokens)] = hi
        in_tab[b, :, pl.ds(tokens, tokens)] = lo
        rows = iota((tokens, LANES), 0).astype(F32)
        hi, lo = split(modes[1, b : b + 1, :] * jnp.exp(-modes[0, b : b + 1, :] * rows))
        out_tab[b, :, pl.ds(0, LANES)] = hi
        out_tab[b, :, pl.ds(LANES, LANES)] = lo
        out_tab[b, :, pl.ds(2 * LANES, LANES)] = hi

    def tables(b, carry):
        at = pl.multiple_of(b * per, per)
        short8 = short_row[pl.ds(at, per), :]
        long8 = long_row[pl.ds(at, per), :]
        for g in range(per):
            turned = pltpu.roll(
                jnp.broadcast_to(short8[g : g + 1, :], (half, tokens)), 0, 1, stride=1, stride_axis=0
            )
            short_tab[b, pl.ds(g * half, half), pl.ds(0, tokens)] = jnp.where(lower, 0.0, turned).astype(BF16)
            short_tab[b, pl.ds(g * half, half), pl.ds(tokens, tokens)] = jnp.where(lower, turned, 0.0).astype(BF16)
            turned = pltpu.roll(
                jnp.broadcast_to(long8[g : g + 1, :], (half, tokens)), half, 1, stride=1, stride_axis=0
            )
            long_tab[b, :, pl.ds(g * tokens, tokens)] = jnp.where(causal, turned, 0.0).astype(BF16)
        return carry

    lax.fori_loop(0, blocks, tables, 0, unroll=2)
    fetches[0].wait()
    fetches[1].wait()

    lane_group = lax.rem(iota((half, 2 * LANES), 1), LANES) // share
    lane_group_tall = lax.rem(iota((tokens, 2 * LANES), 1), LANES) // share

    def windows(x):
        return jnp.concatenate([x[:, :LANES], x[:, LANES:]], 0)

    def short_block(b, carry):
        cols = pl.ds(pl.multiple_of(b * LANES, LANES), LANES)
        pair = jnp.concatenate([ubuf[pl.ds(0, 2 * tokens), cols], ubuf[pl.ds(half, 2 * tokens), cols]], 1)
        full = jnp.dot(short_tab[b], pair, preferred_element_type=F32)
        y = full[:half]
        for g in range(1, per):
            y = jnp.where(lane_group == g, full[g * half : (g + 1) * half], y)
        y = windows(y)
        u = (k_long[:, cols].astype(F32) * q_short[:, cols].astype(F32) * y).astype(BF16)
        ulong[pl.ds(half, tokens), cols] = u
        local = jnp.dot(in_tab[b], jnp.concatenate([u, u], 0), preferred_element_type=F32)
        psend[0, :, cols] = compact(local)
        return carry

    def long_block(b, carry):
        cols = pl.ds(pl.multiple_of(b * LANES, LANES), LANES)
        u = jnp.concatenate([ulong[pl.ds(0, tokens), cols], ulong[pl.ds(half, tokens), cols]], 1)
        wide = jnp.concatenate(
            [jnp.where(lane_group_tall == g, u, jnp.zeros_like(u)) for g in range(per)], 0
        )
        ynear[:, cols] = windows(jnp.dot(long_tab[b], wide, preferred_element_type=F32))
        return carry

    def final_block(b, carry):
        cols = pl.ds(pl.multiple_of(b * LANES, LANES), LANES)
        tall = jnp.where(diag, jnp.concatenate([state[:, cols]] * per, 0), 0.0)
        hi, lo = split(tall)
        far = jnp.dot(out_tab[b], jnp.concatenate([hi, hi, lo], 0), preferred_element_type=F32)
        y = (ynear[:, cols] + far).astype(BF16)
        out[:, cols] = (q_long[:, cols].astype(F32) * y.astype(F32)).astype(BF16)
        return carry

    def scan_copy(k, c, away):
        cols = pl.ds(c * width, width)
        return pltpu.make_async_remote_copy(
            src_ref=psend.at[k, :, cols],
            dst_ref=precv.at[k, :, cols],
            send_sem=scan_send.at[k, c, away],
            recv_sem=scan_recv.at[k, c],
            device_id={"ctx": lax.rem(me + 1 + away, n)},
            device_id_type=MESH,
        )

    def sends(k):
        return lax.rem(me, 2 << k) == (1 << k) - 1

    def scan_send_level(k, c):
        @pl.when(sends(k))
        def _():
            for away in range(1 << k):
                scan_copy(k, c, away).start()

    def scan_take_level(k, c):
        cols = pl.ds(c * width, width)

        @pl.when(lax.rem(me, 2 << k) >= (1 << k))
        def _():
            scan_copy(k, c, 0).wait_recv()
            distance = lax.rem(me, 1 << k) * tokens
            decay = jnp.exp(-lam_rc[:, cols] * distance.astype(F32))
            state[:, cols] = state[:, cols] + decay * precv[k, :, cols]

        if k + 1 < levels:
            decay = jnp.exp(-lam_rc[:, cols] * float(tokens))
            psend[k + 1, :, cols] = psend[0, :, cols] + decay * state[:, cols]

    def over(c, body):
        lax.fori_loop(c * per_chunk, (c + 1) * per_chunk, body, 0, unroll=True)

    def takes(stage):
        for k in range(levels):
            c = stage - 1 - k
            if 0 <= c < chunks:
                scan_take_level(k, c)
                if k + 1 < levels:
                    scan_send_level(k + 1, c)

    state[...] = jnp.zeros_like(state)
    for c in range(chunks):

        @pl.when(me > 0)
        def _():
            halo(c).wait_recv()

        over(c, short_block)
        scan_send_level(0, c)
        takes(c)
    fetches[2].wait()
    nears, ends = 0, 0
    for step in range(levels):
        stage = chunks + step
        goal = -(-chunks * (step + 1) // levels)
        while nears < goal:
            over(nears, long_block)
            nears += 1
        while ends < min(nears, stage - levels):
            over(ends, final_block)
            ends += 1
        takes(stage)
    for c in range(nears, chunks):
        over(c, long_block)
    for c in range(ends, chunks):
        over(c, final_block)

    @pl.when(me < n - 1)
    def _():
        for c in range(chunks):
            halo(c).wait_send()

    for k in range(levels):

        @pl.when(sends(k))
        def _():
            for c in range(chunks):
                for away in range(1 << k):
                    scan_copy(k, c, away).wait_send()


def on_device(n, *args):
    args = args[:6] + (args[6].T, args[7].T)
    q_short, taps, rates = args[0], args[5], args[6]
    tokens, ch = q_short.shape
    order, groups = rates.shape
    blocks = ch // LANES
    per = LANES * groups // ch
    chunks = max(c for c in (1, 2, 4) if blocks % c == 0)
    levels = n.bit_length() - 1
    dma = pltpu.SemaphoreType.DMA
    return pl.pallas_call(
        functools.partial(kernel, n, chunks),
        out_shape=jax.ShapeDtypeStruct((tokens, ch), BF16),
        in_specs=[pl.BlockSpec(memory_space=pl.ANY if i < 5 else pltpu.VMEM) for i in range(8)],
        out_specs=pl.BlockSpec(memory_space=pltpu.VMEM),
        scratch_shapes=[
            pltpu.VMEM((tokens, ch), BF16),
            pltpu.VMEM((tokens, ch), BF16),
            pltpu.VMEM((tokens, ch), BF16),
            pltpu.VMEM((tokens, ch), BF16),
            pltpu.VMEM((tokens, ch), BF16),
            dma((5,)),
            pltpu.VMEM((2 * tokens + tokens // 2, ch), BF16),
            pltpu.VMEM((tokens + tokens // 2, ch), BF16),
            pltpu.VMEM((tokens, ch), F32),
            pltpu.VMEM((blocks, per * tokens // 2, 2 * tokens), BF16),
            pltpu.VMEM((blocks, tokens // 2, per * tokens), BF16),
            pltpu.VMEM((blocks, LANES, 2 * tokens), BF16),
            pltpu.VMEM((blocks, tokens, 3 * LANES), BF16),
            pltpu.VMEM((order, ch), F32),
            pltpu.VMEM((groups, tokens), F32),
            pltpu.VMEM((groups, tokens), F32),
            pltpu.VMEM((2, blocks, LANES), F32),
            pltpu.VMEM((order, ch), F32),
            pltpu.VMEM((levels, order, ch), F32),
            pltpu.VMEM((levels, order, ch), F32),
            dma((chunks,)),
            dma((chunks,)),
            dma((levels, chunks, max(1, n // 2))),
            dma((levels, chunks)),
        ],
        compiler_params=pltpu.CompilerParams(
            collective_id=0, has_side_effects=True, vmem_limit_bytes=60 * 2**20
        ),
    )(*args)


def solution(mesh):
    in_specs = (P("ctx", "ch"),) * 5 + (P(None, "ch"), P("ch", None), P("ch", None))
    return jax.shard_map(
        functools.partial(on_device, mesh.shape["ctx"]),
        mesh=mesh,
        in_specs=in_specs,
        out_specs=P("ctx", "ch"),
        check_vma=False,
    )
```

profile of v0, /device:TPU:29, one launch (start us, length us, event | category | flops | bytes accessed | tf_op | source)
XLA Modules:
  0.0 21.7 jit_solution(4721110997641152640)
XLA Ops:
  0.0 19.9 %shard_map.82 = bf16[128,2048]{1,0:T(8,128)(2,1)} custom-call(bf16[128,2048]{1,0:T(8,128)(2,1)} %q_short_in.1, bf16[128,2048]{1,0:T(8,128)(2,1)} %k_short_in.1, bf16[128,2048]{1,0:T(8,128)(2,1)} %v_input_in.1, bf16[128,2048]{1,0:T(8,128)(2,1)} %q_long_in.1, bf16[128,2048]{1,0:T(8,128)(2,1)} %k_long_in.1, bf16[128,128]{1,0:T(8,128)(2,1)} %taps.1, ...), custom_call_target="tpu_custom_call" | custom-call | tf_op jit(solution)/shard_map/pallas_call | solution.py:293
  19.9 1.9 %copy.10 = bf16[128,2048]{1,0:T(8,128)(2,1)} copy(bf16[128,2048]{1,0:T(8,128)(2,1)} %shard_map.82) | data formatting | bytes 1048576
where the time goes:
time: 22 us; the launch traced here: 21.7 us
  Pallas kernels  19.9 us (90%)
  local copies, waits for them, and re-layouts  1.88 us (9%)
    pallas_call x1, Pallas kernels, on_device(): pl.pallas_call(functools.partial(kernel, n, chunks), out_shape=jax.ShapeD...  19.9 us
    unnamed x1, local copies, waits for them, and re-layouts  1.88 us

commit v1 on v0

--- a/solution.py
+++ b/solution.py
@@ -282,6 +282,7 @@
 
 def on_device(n, *args):
     args = args[:6] + (args[6].T, args[7].T)
+    args = tuple(pltpu.with_memory_space_constraint(a, pltpu.HBM) for a in args)
     q_short, taps, rates = args[0], args[5], args[6]
     tokens, ch = q_short.shape
     order, groups = rates.shape
@@ -293,7 +294,7 @@
     return pl.pallas_call(
         functools.partial(kernel, n, chunks),
         out_shape=jax.ShapeDtypeStruct((tokens, ch), BF16),
-        in_specs=[pl.BlockSpec(memory_space=pl.ANY if i < 5 else pltpu.VMEM) for i in range(8)],
+        in_specs=[pl.BlockSpec(memory_space=pltpu.HBM if i < 5 else pltpu.VMEM) for i in range(8)],
         out_specs=pl.BlockSpec(memory_space=pltpu.VMEM),
         scratch_shapes=[
             pltpu.VMEM((tokens, ch), BF16),
@@ -322,7 +323,7 @@
             dma((levels, chunks)),
         ],
         compiler_params=pltpu.CompilerParams(
-            collective_id=0, has_side_effects=True, vmem_limit_bytes=60 * 2**20
+            collective_id=0, has_side_effects=True, vmem_limit_bytes=40 * 2**20
         ),
     )(*args)
 

time: 22 us -> 20.1 us (0.914)
  local copies, waits for them, and re-layouts: 1.88 us -> 0.8 us
  Pallas kernels: 19.9 us -> 19.1 us
    unnamed x1, local copies, waits for them, and re-layouts: 1.88 us -> 0.8 us
    pallas_call x1, Pallas kernels: 19.9 us -> 19.1 us  [on_device(): pl.pallas_call(functools.partial(kernel, n, chunks), out_shape=jax.ShapeD...]
where the time goes in v1:
time: 20.1 us; the launch traced here: 19.9 us
  Pallas kernels  19.1 us (95%)
  local copies, waits for them, and re-layouts  0.8 us (4%)
    pallas_call x1, Pallas kernels, on_device(): pl.pallas_call(functools.partial(kernel, n, chunks), out_shape=jax.ShapeD...  19.1 us
    unnamed x1, local copies, waits for them, and re-layouts  0.8 us

profile of v1, /device:TPU:29, one launch (start us, length us, event | category | flops | bytes accessed | tf_op | source)
XLA Modules:
  0.0 19.9 jit_solution(16519670931444797453)
XLA Ops:
  0.0 19.1 %shard_map.82 = bf16[128,2048]{1,0:T(8,128)(2,1)S(1)} custom-call(bf16[128,2048]{1,0:T(8,128)(2,1)} %q_short_in.1, bf16[128,2048]{1,0:T(8,128)(2,1)} %k_short_in.1, bf16[128,2048]{1,0:T(8,128)(2,1)} %v_input_in.1, bf16[128,2048]{1,0:T(8,128)(2,1)} %q_long_in.1, bf16[128,2048]{1,0:T(8,128)(2,1)} %k_long_in.1, bf16[128,128]{1,0:T(8,128)(2,1)} %taps.1, ...), custom_call_target="tpu_custom_call" | custom-call | tf_op jit(solution)/shard_map/pallas_call | solution.py:294
  19.1 0.8 %copy.10 = bf16[128,2048]{1,0:T(8,128)(2,1)} copy(bf16[128,2048]{1,0:T(8,128)(2,1)S(1)} %shard_map.82) | data formatting | bytes 1048576

commit v2 on v1

v2 whole, which is shorter than its diff:
```python
import functools
import math

import jax
import jax.numpy as jnp
from jax import lax
from jax.experimental import pallas as pl
from jax.experimental.pallas import tpu as pltpu
from jax.sharding import PartitionSpec as P

MESH = pl.DeviceIdType.MESH
LANES = 128
F32 = jnp.float32
BF16 = jnp.bfloat16
LOG2E = math.log2(math.e)
LAG = 3


def iota(shape, dim):
    return lax.broadcasted_iota(jnp.int32, shape, dim)


def split(x):
    hi = x.astype(BF16)
    return hi, (x - hi.astype(F32)).astype(BF16)


def kernel(
    n, chunks, q_short_in, k_short_in, v_input_in, q_long_in, k_long_in, taps_in, rates_in, weights_in, out,
    q_short, q_long, k_long, k_short, v_input, taps, rates, weights, fetch_sem, early_sem,
    ubuf, ulong, ynear, short_tab, long_tab, out_tab, masks, lam_rc, short_row, wide_sums, wide_pairs, modes,
    state, plocal, psend, precv, halo_send, halo_recv, swap_send, scan_send, scan_recv,
):
    me = lax.axis_index("ctx")
    tokens, ch = k_short.shape
    half = tokens // 2
    order, groups = rates.shape
    share = ch // groups
    per = LANES // share
    blocks = ch // LANES
    per_chunk = blocks // chunks
    width = per_chunk * LANES
    levels = n.bit_length() - 1
    parts = 2 if chunks % 2 == 0 else 1

    def early(i, part):
        source, target = ((k_short_in, k_short), (v_input_in, v_input))[i]
        cols = pl.ds(part * (ch // parts), ch // parts)
        return pltpu.make_async_copy(source.at[:, cols], target.at[:, cols], early_sem.at[i, part])

    fetches = [
        pltpu.make_async_copy(source, target, fetch_sem.at[i])
        for i, (source, target) in enumerate(
            (
                (taps_in, taps),
                (rates_in, rates),
                (weights_in, weights),
                (k_long_in, k_long),
                (q_short_in, q_short),
                (q_long_in, q_long),
            )
        )
    ]
    for part in range(parts):
        for i in range(2):
            early(i, part).start()

    barrier = pltpu.get_barrier_semaphore()
    for step in range(1, n):
        pl.semaphore_signal(
            barrier, inc=1, device_id={"ctx": lax.rem(me + step, n)}, device_id_type=MESH
        )
    for fetch in fetches:
        fetch.start()

    def halo(c, count=1):
        at = pl.ds(c * per_chunk, count * per_chunk)
        return pltpu.make_async_remote_copy(
            src_ref=ubuf.at[at, pl.ds(tokens, tokens), :],
            dst_ref=ubuf.at[at, pl.ds(0, tokens), :],
            send_sem=halo_send,
            recv_sem=halo_recv.at[c],
            device_id={"ctx": lax.rem(me + 1, n)},
            device_id_type=MESH,
        )

    for c in range(chunks):
        if c % (chunks // parts) == 0:
            for i in range(2):
                early(i, c // (chunks // parts)).wait()
        for b in range(c * per_chunk, (c + 1) * per_chunk):
            cols = pl.ds(b * LANES, LANES)
            ubuf[b, pl.ds(tokens, tokens), :] = (k_short[:, cols].astype(F32) * v_input[:, cols].astype(F32)).astype(BF16)
        if c == 0:
            pl.semaphore_wait(barrier, n - 1)

        @pl.when(me < n - 1)
        def _():
            halo(c).start()

    @pl.when(me == 0)
    def _():
        ubuf[:, pl.ds(0, tokens), :] = jnp.zeros((blocks, tokens, LANES), BF16)

    state[...] = jnp.zeros_like(state)

    for i in range(3):
        fetches[i].wait()
    rate = rates[...] * LOG2E
    scaled = weights[...] * jnp.sqrt(2.0 * rates[...])
    own = lax.rem(iota((groups, LANES), 0), per) == iota((groups, LANES), 1) // order

    def wide(x):
        x = jnp.transpose(jnp.concatenate([x, jnp.zeros((LANES - order, groups), F32)], 0))
        shift = order
        while shift < LANES:
            x = x + pltpu.roll(x, shift, 1)
            shift *= 2
        return jnp.where(own, x, 0.0)

    modes[0] = jnp.sum(wide(rate).reshape(blocks, per, LANES), axis=1)
    scaled_wide = wide(scaled)
    modes[1] = jnp.sum(scaled_wide.reshape(blocks, per, LANES), axis=1)
    wide_sums[...] = jnp.broadcast_to(jnp.sum(scaled_wide, axis=1, keepdims=True), (groups, LANES))
    hi = scaled_wide.astype(BF16).astype(F32)
    wide_pairs[...] = jnp.concatenate(
        [hi.reshape(blocks, per, LANES), (scaled_wide - hi).reshape(blocks, per, LANES)], 1
    ).astype(BF16)
    flip = (lax.rem(iota((tokens, tokens), 0) + iota((tokens, tokens), 1), tokens) == 0).astype(BF16)
    taps_t = jnp.transpose(taps[...].astype(F32)).astype(BF16)
    short_row[...] = jnp.dot(taps_t, flip, preferred_element_type=F32)

    ahead = -(tokens - iota((order, tokens), 1)).astype(F32)
    rows = -iota((tokens, LANES), 0).astype(F32)
    lane_block = iota((order, LANES), 1) // share
    first_lane = iota((per, tokens), 1) == 0
    rows_half = iota((half, tokens), 0)
    masks[0] = (rows_half < iota((half, tokens), 1)).astype(F32)
    masks[1] = (rows_half >= iota((half, tokens), 1)).astype(F32)
    masks[2] = (rows_half + half >= iota((half, tokens), 1)).astype(F32)
    diag = iota((LANES, LANES), 0) // order == iota((LANES, LANES), 1) // share

    def turn(row, shift):
        return pltpu.roll(jnp.broadcast_to(row, (half, tokens)), shift, 1, stride=1, stride_axis=0)

    def early_tables(b):
        lam = jnp.zeros((order, LANES), F32)
        for g in range(per):
            column = jnp.broadcast_to(rate[:, b * per + g : b * per + g + 1], (order, tokens))
            lam = jnp.where(lane_block == g, column, lam)
            hi, lo = split(jnp.exp2(column * ahead))
            long_tab[b, g, pl.ds(half, order), :] = hi
            long_tab[b, g, pl.ds(half + order, order), :] = lo
        lam_rc[:, pl.ds(b * LANES, LANES)] = lam
        for g in range(per):
            turned = turn(short_row[pl.ds(b * per + g, 1), :], 0)
            for side in range(2):
                short_tab[b, side, pl.ds(g * half, half), :] = (turned * masks[side]).astype(BF16)

    def late_tables(b):
        parts = [
            jnp.concatenate([long_tab[b, g, pl.ds(half + i * order, order), :] for g in range(per)], 0)
            for i in range(2)
        ]
        both = jnp.dot(wide_pairs[b], jnp.concatenate(parts, 1), preferred_element_type=F32)
        long8 = both[:per, :tokens] + both[:per, tokens:] + both[per:, :tokens]
        long8 = jnp.where(first_lane, wide_sums[pl.ds(b * per, per), :], long8)
        for g in range(per):
            long_tab[b, g, pl.ds(0, half), :] = (turn(long8[g : g + 1, :], half) * masks[2]).astype(BF16)
        out_tab[b] = (modes[1, pl.ds(b, 1), :] * jnp.exp2(modes[0, pl.ds(b, 1), :] * rows)).astype(BF16)

    lane_group = lax.rem(iota((half, 2 * LANES), 1), LANES) // share
    lane_group_tall = lax.rem(iota((tokens, 2 * LANES), 1), LANES) // share

    def windows(x):
        return jnp.concatenate([x[:, :LANES], x[:, LANES:]], 0)

    def short_blocks(bs):
        reach = tokens + half
        fulls = []
        for b in bs:
            pair = jnp.concatenate([ubuf[b, pl.ds(0, reach), :], ubuf[b, pl.ds(half, reach), :]], 1)
            table = jnp.concatenate([short_tab[b, 0], short_tab[b, 1][:, :half]], 1)
            fulls.append(jnp.dot(table, pair, preferred_element_type=F32))
        for b, full in zip(bs, fulls):
            cols = pl.ds(b * LANES, LANES)
            y = full[:half]
            for g in range(1, per):
                y = jnp.where(lane_group == g, full[g * half : (g + 1) * half], y)
            y = windows(y)
            ulong[b] = (k_long[:, cols].astype(F32) * q_short[:, cols].astype(F32) * y).astype(BF16)

    def long_blocks(bs):
        for b in bs:
            cols = pl.ds(b * LANES, LANES)
            u = ulong[b]
            u = jnp.concatenate([jnp.concatenate([jnp.zeros_like(u[:half]), u[:half]], 0), u], 1)
            tall = jnp.concatenate(
                [jnp.where(lane_group_tall == g, u, jnp.zeros_like(u)) for g in range(per)], 0
            )
            table = jnp.concatenate([long_tab[b, g] for g in range(per)], 1)
            full = jnp.dot(table, tall, preferred_element_type=F32)
            ynear[:, cols] = windows(full[:half])
            local = full[half : half + order, LANES:] + full[half + order :, LANES:]
            plocal[:, cols] = local
            psend[0, :, cols] = local.astype(BF16)

    def final_blocks(bs):
        for b in bs:
            cols = pl.ds(b * LANES, LANES)
            both = [jnp.concatenate([x] * per, 0) for x in split(state[:, cols])]
            tall = jnp.concatenate([jnp.where(diag, x, jnp.zeros_like(x)) for x in both], 0)
            table = out_tab[b]
            far = jnp.dot(jnp.concatenate([table, table], 1), tall, preferred_element_type=F32)
            y = (ynear[:, cols] + far).astype(BF16)
            out[:, cols] = (q_long[:, cols].astype(F32) * y.astype(F32)).astype(BF16)

    def members(c):
        return range(c * per_chunk, (c + 1) * per_chunk)

    def exchange(c, count=1):
        cols = pl.ds(c * width, count * width)
        return pltpu.make_async_remote_copy(
            src_ref=psend.at[0, :, cols],
            dst_ref=precv.at[0, :, cols],
            send_sem=swap_send,
            recv_sem=scan_recv.at[0, c],
            device_id={"ctx": me + 1 - 2 * lax.rem(me, 2)},
            device_id_type=MESH,
        )

    def scan_copy(k, c, away, count=1):
        cols = pl.ds(c * width, count * width)
        return pltpu.make_async_remote_copy(
            src_ref=psend.at[k, :, cols],
            dst_ref=precv.at[k, :, cols],
            send_sem=scan_send.at[away],
            recv_sem=scan_recv.at[k, c],
            device_id={"ctx": lax.rem(me + 2 + away, n)},
            device_id_type=MESH,
        )

    def sends(k):
        return lax.rem(me, 2 << k) == (1 << k) - 2

    def early_take(c):
        cols = pl.ds(c * width, width)
        for j in range(1, levels):

            @pl.when(sends(j))
            def _():
                exchange(c).wait_recv()
                lam = lam_rc[:, cols]
                total = jnp.exp2(-lam * float(tokens)) * plocal[:, cols] + precv[0, :, cols].astype(F32)
                if j > 1:
                    ahead_of = jnp.zeros((order, width), F32)
                    for k in range(1, j):
                        scan_copy(k, c, 0).wait_recv()
                        decay = jnp.exp2(-lam * float(((1 << k) - 2) * tokens))
                        ahead_of = ahead_of + decay * precv[k, :, cols].astype(F32)
                    state[:, cols] = ahead_of
                    total = total + jnp.exp2(-lam * float(2 * tokens)) * ahead_of
                psend[j, :, cols] = total.astype(BF16)
                for away in range(1 << j):
                    scan_copy(j, c, away).start()

    def late_take(c):
        cols = pl.ds(c * width, width)

        @pl.when(lax.rem(me, 2) == 1)
        def _():
            exchange(c).wait_recv()
            state[:, cols] = state[:, cols] + precv[0, :, cols].astype(F32)

        for k in range(1, levels):
            place = lax.rem(me, 2 << k)

            @pl.when(jnp.logical_and(place >= 1 << k, jnp.logical_or(place != (2 << k) - 2, me == n - 2)))
            def _():
                scan_copy(k, c, 0).wait_recv()
                distance = lax.rem(me, 1 << k) * tokens
                decay = jnp.exp2(-lam_rc[:, cols] * distance.astype(F32))
                state[:, cols] = state[:, cols] + decay * precv[k, :, cols].astype(F32)

    for b in members(0):
        early_tables(b)
    fetches[3].wait()
    fetches[4].wait()

    def after_long(c):
        @pl.when(me < n - 1)
        def _():
            exchange(c).start()

    for c in range(chunks):
        last = c == chunks - 1
        if c >= LAG:
            early_take(c - LAG)
        if last and c > 0:
            long_blocks(members(c - 1))
            after_long(c - 1)

        @pl.when(me > 0)
        def _():
            halo(c).wait_recv()

        short_blocks(members(c))
        for b in members(c):
            late_tables(b)
        if not last:
            for b in members(c + 1):
                early_tables(b)
            if c > 0:
                long_blocks(members(c - 1))
                after_long(c - 1)

    long_blocks(members(chunks - 1))
    after_long(chunks - 1)
    for c in range(max(0, chunks - LAG), chunks):
        early_take(c)
    fetches[5].wait()
    for c in range(chunks):
        late_take(c)
        final_blocks(members(c))

    @pl.when(me < n - 1)
    def _():
        halo(0, chunks).wait_send()
        exchange(0, chunks).wait_send()

    for k in range(1, levels):

        @pl.when(sends(k))
        def _():
            for away in range(1 << k):
                scan_copy(k, 0, away, chunks).wait_send()


def on_device(n, *args):
    args = args[:6] + (args[6].T, args[7].T)
    args = tuple(pltpu.with_memory_space_constraint(a, pltpu.HBM) for a in args)
    q_short, taps, rates = args[0], args[5], args[6]
    tokens, ch = q_short.shape
    order, groups = rates.shape
    blocks = ch // LANES
    per = LANES * groups // ch
    chunks = max(c for c in (1, 2, 4, 8) if blocks % c == 0)
    levels = n.bit_length() - 1
    dma = pltpu.SemaphoreType.DMA
    return pl.pallas_call(
        functools.partial(kernel, n, chunks),
        out_shape=jax.ShapeDtypeStruct((tokens, ch), BF16),
        in_specs=[pl.BlockSpec(memory_space=pltpu.HBM)] * 8,
        out_specs=pl.BlockSpec(memory_space=pltpu.VMEM),
        scratch_shapes=[
            pltpu.VMEM((tokens, ch), BF16),
            pltpu.VMEM((tokens, ch), BF16),
            pltpu.VMEM((tokens, ch), BF16),
            pltpu.VMEM((tokens, ch), BF16),
            pltpu.VMEM((tokens, ch), BF16),
            pltpu.VMEM(taps.shape, BF16),
            pltpu.VMEM((order, groups), F32),
            pltpu.VMEM((order, groups), F32),
            dma((6,)),
            dma((2, 2)),
            pltpu.VMEM((blocks, 2 * tokens, LANES), BF16),
            pltpu.VMEM((blocks, tokens, LANES), BF16),
            pltpu.VMEM((tokens, ch), F32),
            pltpu.VMEM((blocks, 2, per * tokens // 2, tokens), BF16),
            pltpu.VMEM((blocks, per, tokens // 2 + 2 * order, tokens), BF16),
            pltpu.VMEM((blocks, tokens, LANES), BF16),
            pltpu.VMEM((3, tokens // 2, tokens), F32),
            pltpu.VMEM((order, ch), F32),
            pltpu.VMEM((groups, tokens), F32),
            pltpu.VMEM((groups, LANES), F32),
            pltpu.VMEM((blocks, 2 * per, LANES), BF16),
            pltpu.VMEM((2, blocks, LANES), F32),
            pltpu.VMEM((order, ch), F32),
            pltpu.VMEM((order, ch), F32),
            pltpu.VMEM((levels, order, ch), BF16),
            pltpu.VMEM((levels, order, ch), BF16),
            dma,
            dma((chunks,)),
            dma,
            dma((max(1, n // 2),)),
            dma((levels, chunks)),
        ],
        compiler_params=pltpu.CompilerParams(
            collective_id=0, has_side_effects=True, vmem_limit_bytes=40 * 2**20
        ),
    )(*args)


def solution(mesh):
    in_specs = (P("ctx", "ch"),) * 5 + (P(None, "ch"), P("ch", None), P("ch", None))
    return jax.shard_map(
        functools.partial(on_device, mesh.shape["ctx"]),
        mesh=mesh,
        in_specs=in_specs,
        out_specs=P("ctx", "ch"),
        check_vma=False,
    )
```

time: 20.1 us -> 16.8 us (0.84)
  Pallas kernels: 19.1 us -> 15.8 us
    pallas_call x1, Pallas kernels: 19.1 us -> 15.8 us  [on_device(): pl.pallas_call(functools.partial(kernel, n, chunks), out_shape=jax.ShapeD...]
where the time goes in v2:
time: 16.8 us; the launch traced here: 16.6 us
  Pallas kernels  15.8 us (94%)
  local copies, waits for them, and re-layouts  0.8 us (5%)
    pallas_call x1, Pallas kernels, on_device(): pl.pallas_call(functools.partial(kernel, n, chunks), out_shape=jax.ShapeD...  15.8 us
    unnamed x1, local copies, waits for them, and re-layouts  0.8 us

profile of v2, /device:TPU:29, one launch (start us, length us, event | category | flops | bytes accessed | tf_op | source)
XLA Modules:
  0.0 16.6 jit_solution(13913659524975069391)
XLA Ops:
  0.0 15.8 %shard_map.82 = bf16[128,2048]{1,0:T(8,128)(2,1)S(1)} custom-call(bf16[128,2048]{1,0:T(8,128)(2,1)} %q_short_in.1, bf16[128,2048]{1,0:T(8,128)(2,1)} %k_short_in.1, bf16[128,2048]{1,0:T(8,128)(2,1)} %v_input_in.1, bf16[128,2048]{1,0:T(8,128)(2,1)} %q_long_in.1, bf16[128,2048]{1,0:T(8,128)(2,1)} %k_long_in.1, bf16[128,128]{1,0:T(8,128)(2,1)} %taps_in.1, ...), custom_call_target="tpu_custom_call" | custom-call | tf_op jit(solution)/shard_map/pallas_call | solution.py:350
  15.8 0.8 %copy.10 = bf16[128,2048]{1,0:T(8,128)(2,1)} copy(bf16[128,2048]{1,0:T(8,128)(2,1)S(1)} %shard_map.82) | data formatting | bytes 1048576

commit v3 on v2

v3 whole, which is shorter than its diff:
```python
import functools
import math

import jax
import jax.numpy as jnp
from jax import lax
from jax.experimental import pallas as pl
from jax.experimental.pallas import tpu as pltpu
from jax.sharding import PartitionSpec as P

MESH = pl.DeviceIdType.MESH
LANES = 128
F32 = jnp.float32
BF16 = jnp.bfloat16
LOG2E = math.log2(math.e)
WINDOWS = 4
SPANS = 8
BLOCK = 8


def iota(shape, dim):
    return lax.broadcasted_iota(jnp.int32, shape, dim)


def split(x):
    hi = x.astype(BF16)
    return hi, (x - hi.astype(F32)).astype(BF16)


def kernel(
    n, chunks, q_short_in, k_short_in, v_input_in, q_long_in, k_long_in, taps_in, rates_in, weights_in, out,
    q_short, q_long, k_long, k_short, v_input, taps, rates, weights, fetch_sem, early_sem,
    ubuf, ulong, ynear, short_tab, long_tab, out_tab, masks, long_mask, lam_rc, short_row, modes,
    turned_modes, state, inner, plocal, psend, precv, ready, halo_send, halo_recv, swap_send, chip_send, relay_send, last_send, block_send, scan_recv,
):
    me = lax.axis_index("ctx")
    tokens, ch = k_short.shape
    size = tokens // WINDOWS
    tap_rows = tokens // SPANS
    order, groups = rates.shape
    share = ch // groups
    per = LANES // share
    blocks = ch // LANES
    per_chunk = blocks // chunks
    width = per_chunk * LANES
    levels = n.bit_length() - 1
    chips = min(n, BLOCK) // 2
    odd = lax.rem(me, 2)
    chip = lax.rem(me, 2 * chips) // 2
    first_level = (2 * chips).bit_length() - 1
    bounds = sorted({chunks // 2, chunks - chunks // 4, chunks} - {0})
    bounds = list(zip([0] + bounds[:-1], bounds))
    final = len(bounds) - 1
    parts = 2 if chunks % 2 == 0 else 1

    def early(i, part):
        source, target = ((k_short_in, k_short), (v_input_in, v_input))[i]
        cols = pl.ds(part * (ch // parts), ch // parts)
        return pltpu.make_async_copy(source.at[:, cols], target.at[:, cols], early_sem.at[i, part])

    fetches = [
        pltpu.make_async_copy(source, target, fetch_sem.at[i])
        for i, (source, target) in enumerate(
            (
                (taps_in, taps),
                (rates_in, rates),
                (weights_in, weights),
                (k_long_in, k_long),
                (q_short_in, q_short),
                (q_long_in, q_long),
            )
        )
    ]
    for part in range(parts):
        for i in range(2):
            early(i, part).start()

    barrier = pltpu.get_barrier_semaphore()

    def signal(semaphore, device):
        pl.semaphore_signal(
            semaphore, inc=1, device_id={"ctx": lax.rem(device + n, n)}, device_id_type=MESH
        )

    if n > BLOCK:
        for step in range(1, n):
            signal(barrier, me + step)
    else:
        signal(barrier, me + 1 - 2 * odd)

        @pl.when(jnp.logical_and(odd == 0, me > 0))
        def _():
            signal(barrier, me - 1)

        for step in range(1, chips):

            @pl.when(chip + step < chips)
            def _():
                for core in range(2):
                    signal(barrier, me - odd + 2 * step + core)

    for fetch in fetches:
        fetch.start()

    def halo(c, count=1):
        at = pl.ds(c * per_chunk, count * per_chunk)
        return pltpu.make_async_remote_copy(
            src_ref=ubuf.at[at, pl.ds(tokens, tokens), :],
            dst_ref=ubuf.at[at, pl.ds(0, tokens), :],
            send_sem=halo_send,
            recv_sem=halo_recv.at[c],
            device_id={"ctx": lax.rem(me + 1, n)},
            device_id_type=MESH,
        )

    for c in range(chunks):
        if c % (chunks // parts) == 0:
            for i in range(2):
                early(i, c // (chunks // parts)).wait()
        for b in range(c * per_chunk, (c + 1) * per_chunk):
            cols = pl.ds(b * LANES, LANES)
            ubuf[b, pl.ds(tokens, tokens), :] = (k_short[:, cols].astype(F32) * v_input[:, cols].astype(F32)).astype(BF16)
        if c == 0 and n > BLOCK:
            pl.semaphore_wait(barrier, n - 1)
        elif c == 0:
            ahead_of = jnp.logical_and(odd == 1, me < n - 1).astype(jnp.int32)
            pl.semaphore_wait(barrier, 1 + 2 * chip + ahead_of)

        @pl.when(me < n - 1)
        def _():
            halo(c).start()

    if n <= BLOCK:
        for step in range(1, chips):

            @pl.when(chip >= step)
            def _():
                for core in range(2):
                    signal(ready, me - odd - 2 * step + core)

    @pl.when(me == 0)
    def _():
        ubuf[:, pl.ds(0, tokens), :] = jnp.zeros((blocks, tokens, LANES), BF16)

    state[...] = jnp.zeros_like(state)

    for i in range(3):
        fetches[i].wait()
    rate = rates[...] * LOG2E
    scaled = weights[...] * jnp.sqrt(2.0 * rates[...])
    for i, x in enumerate((rate, scaled)):
        turned_modes[i] = jnp.transpose(jnp.concatenate([x, jnp.zeros((LANES - order, groups), F32)], 0))
    for i in range(2):
        row = turned_modes[i, pl.ds(0, blocks, stride=per), :]
        for g in range(1, per):
            row = row + pltpu.roll(turned_modes[i, pl.ds(g, blocks, stride=per), :], g * order, 1)
        modes[i] = row
    flip = (lax.rem(iota((tokens, tokens), 0) + iota((tokens, tokens), 1), tokens) == 0).astype(BF16)
    taps_t = jnp.transpose(taps[...].astype(F32)).astype(BF16)
    short_row[...] = jnp.dot(taps_t, flip, preferred_element_type=F32)

    lane = iota((order, LANES), 1)
    ahead = (lax.rem(lane, size) - size).astype(F32)
    first = lax.rem(lane, size) == 0
    first_row = lax.rem(iota((1, LANES), 1), size) == 0
    rows = -iota((size, LANES), 0).astype(F32)
    masks[0] = (iota((tap_rows, tokens), 0) < iota((tap_rows, tokens), 1)).astype(F32)
    masks[1] = (iota((tap_rows, tokens), 0) >= iota((tap_rows, tokens), 1)).astype(F32)
    long_mask[...] = (iota((size, LANES), 0) >= lax.rem(iota((size, LANES), 1), size)).astype(F32)
    def turn(row, count, shift):
        return pltpu.roll(jnp.broadcast_to(row, (count, LANES)), shift, 1, stride=1, stride_axis=0)

    def spread(x, start, count):
        at = start // LANES * LANES
        x = x[:, at : at + LANES]
        if x.shape[1] < LANES:
            x = jnp.concatenate([x, jnp.zeros((order, LANES - x.shape[1]), F32)], 1)
        return jnp.take_along_axis(x, start - at + lane // (LANES // count), axis=1)

    def make_tables(b):
        for g in range(per):
            turned = turn(short_row[pl.ds(b * per + g, 1), :], tap_rows, 0)
            for side in range(2):
                short_tab[b, side, pl.ds(g * tap_rows, tap_rows), :] = (turned * masks[side]).astype(BF16)
        for j in range(per // WINDOWS):
            start = b * per + j * WINDOWS
            table = jnp.exp2(spread(rate, start, WINDOWS) * ahead)
            hi, lo = split(table)
            long_tab[b, j, pl.ds(size, order), :] = hi
            long_tab[b, j, pl.ds(size + order, order), :] = lo
            row = jnp.sum(spread(scaled, start, WINDOWS) * jnp.where(first, 1.0, table), axis=0, keepdims=True)
            row = jnp.where(first_row, pltpu.roll(row, size, 1), row)
            long_tab[b, j, pl.ds(0, size), :] = (turn(row, size, LANES - size) * long_mask[...]).astype(BF16)
        lam_rc[:, pl.ds(b * LANES, LANES)] = spread(rate, b * per, per)
        out_tab[b] = (modes[1, pl.ds(b, 1), :] * jnp.exp2(modes[0, pl.ds(b, 1), :] * rows)).astype(BF16)

    lane_group = lax.rem(iota((tap_rows, SPANS * LANES), 1), LANES) // share
    lane_group_tall = lax.rem(iota((size, WINDOWS * LANES), 1), LANES) // share

    lane_group_order = lax.rem(iota((order, WINDOWS * LANES), 1), LANES) // share

    def stacked(x):
        return jnp.concatenate([x[:, i : i + LANES] for i in range(0, x.shape[1], LANES)], 0)

    def beside(x):
        return jnp.concatenate([x[i : i + size] for i in range(0, tokens, size)], 1)

    def short_blocks(bs):
        reach = tokens + tap_rows
        fulls = []
        for b in bs:
            spans = jnp.concatenate([ubuf[b, pl.ds(w * tap_rows, reach), :] for w in range(SPANS)], 1)
            table = jnp.concatenate([short_tab[b, 0], short_tab[b, 1][:, :tap_rows]], 1)
            fulls.append(jnp.dot(table, spans, preferred_element_type=F32))
        for b, full in zip(bs, fulls):
            cols = pl.ds(b * LANES, LANES)
            y = full[:tap_rows]
            for g in range(1, per):
                y = jnp.where(lane_group == g, full[g * tap_rows : (g + 1) * tap_rows], y)
            y = stacked(y)
            ulong[b] = (k_long[:, cols].astype(F32) * q_short[:, cols].astype(F32) * y).astype(BF16)

    def pieces(x):
        return [x[:, i : i + LANES] for i in range(0, x.shape[1], LANES)]

    def long_blocks(bs):
        for b in bs:
            cols = pl.ds(b * LANES, LANES)
            u = beside(ulong[b])
            tall = jnp.concatenate(
                [jnp.where(lane_group_tall == g, u, jnp.zeros_like(u)) for g in range(per)], 0
            )
            table = jnp.concatenate([long_tab[b, j] for j in range(per // WINDOWS)], 1)
            full = jnp.dot(table, tall, preferred_element_type=F32)
            ynear[b] = full[:size]
            local = full[size : size + order] + full[size + order :]
            inner[b] = local
            decay = jnp.exp2(-lam_rc[:, cols] * float(size))
            total = local[:, :LANES]
            for piece in pieces(local)[1:]:
                total = decay * total + piece
            plocal[:, cols] = total
            psend[0, :, cols] = total.astype(BF16)

    def final_blocks(bs):
        for b in bs:
            cols = pl.ds(b * LANES, LANES)
            decay = jnp.exp2(-lam_rc[:, cols] * float(size))
            starts = [state[:, cols]]
            for piece in pieces(inner[b])[:-1]:
                starts.append(decay * starts[-1] + piece)
            tall = jnp.concatenate(
                [
                    jnp.where(lane_group_order == g, x, jnp.zeros_like(x))
                    for x in split(jnp.concatenate(starts, 1))
                    for g in range(per)
                ],
                0,
            )
            table = out_tab[b]
            far = jnp.dot(jnp.concatenate([table, table], 1), tall, preferred_element_type=F32)
            y = stacked(ynear[b] + far).astype(BF16)
            out[:, cols] = (q_long[:, cols].astype(F32) * y.astype(F32)).astype(BF16)

    def members(c):
        return range(c * per_chunk, (c + 1) * per_chunk)

    def columns(g, to=None):
        start, stop = bounds[g][0] * width, bounds[g if to is None else to][1] * width
        return pl.ds(start, stop - start)

    def send(source, target, g, send_sem, device, to=None):
        cols = columns(g, to)
        return pltpu.make_async_remote_copy(
            src_ref=psend.at[source, :, cols],
            dst_ref=precv.at[target, :, cols],
            send_sem=send_sem,
            recv_sem=scan_recv.at[target, g],
            device_id={"ctx": lax.rem(device, n)},
            device_id_type=MESH,
        )

    def swap(g, to=None):
        return send(0, 0, g, swap_send, me + 1 - 2 * odd, to)

    def chip_copy(g, step, to=None):
        return send(1, 1 + chip, g, chip_send.at[step - 1], me + 2 * step - 1, to)

    def relay(g, to=None):
        return send(2, chips, g, relay_send, me + 1, to)

    def last_copy(step, core):
        return send(1, 1 + chip, final, last_send.at[step - 1, core], me + 2 * step + core)

    def block_copy(k, g, away, to=None):
        return send(3, chips + 1 + k - first_level, g, block_send.at[away], me + 2 + away, to)

    def arrived(slot, g):
        send(0, slot, g, swap_send, me + 1).wait_recv()
        return precv[slot, :, columns(g)].astype(F32)

    def decayed(g, distance):
        return jnp.exp2(-lam_rc[:, columns(g)] * distance)

    def in_later_chip(step):
        return chip + step < chips

    def group_done(g):
        both_ways = jnp.logical_or(odd == 0, chip < chips - 1) if n <= BLOCK else odd >= 0
        one_way = odd == 0 if n <= BLOCK else jnp.logical_or(odd == 0, chip == chips - 1)

        @pl.when(both_ways if g == final else one_way)
        def _():
            swap(g).start()

    def odd_send(g):
        @pl.when(jnp.logical_and(odd == 1, chip < chips - 1))
        def _():
            total = decayed(g, float(tokens)) * arrived(0, g) + plocal[:, columns(g)]
            psend[1, :, columns(g)] = total.astype(BF16)
            for step in range(1, chips):

                @pl.when(in_later_chip(step))
                def _():
                    chip_copy(g, step).start()

    def even_send_last():
        @pl.when(jnp.logical_and(odd == 0, chip < chips - 1))
        def _():
            total = decayed(final, float(tokens)) * plocal[:, columns(final)] + arrived(0, final)
            psend[1, :, columns(final)] = total.astype(BF16)
            for step in range(1, chips):

                @pl.when(in_later_chip(step))
                def _():
                    for core in range(2):
                        last_copy(step, core).start()

    def take_chips(g, cores):
        cols = columns(g)
        for source in range(chips - 1):

            @pl.when(jnp.logical_and(chip > source, odd < cores))
            def _():
                distance = ((chip - source - 1) * 2 + odd) * tokens
                state[:, cols] = state[:, cols] + decayed(g, distance.astype(F32)) * arrived(1 + source, g)

    def take(g):
        cols = columns(g)
        take_chips(g, 1 if g < final else 2)
        if g < final:

            @pl.when(jnp.logical_and(odd == 0, chip > 0))
            def _():
                psend[2, :, cols] = state[:, cols].astype(BF16)
                relay(g).start()

            @pl.when(jnp.logical_and(odd == 1, chip > 0))
            def _():
                state[:, cols] = decayed(g, float(tokens)) * arrived(chips, g)

        @pl.when(jnp.logical_and(odd == 1, jnp.logical_or(chip == chips - 1, g == final)))
        def _():
            send(0, 0, g, swap_send, me + 1).wait_recv()

        @pl.when(odd == 1)
        def _():
            state[:, cols] = state[:, cols] + precv[0, :, cols].astype(F32)

        if n > BLOCK:
            last_even = jnp.logical_and(odd == 0, chip == chips - 1)

            @pl.when(last_even)
            def _():
                send(0, 0, g, swap_send, me + 1).wait_recv()

            for k in range(first_level, levels):

                @pl.when(lax.rem(me, 2 << k) >= 1 << k)
                def _():
                    distance = lax.rem(me, 1 << k) * tokens
                    slot = chips + 1 + k - first_level
                    state[:, cols] = state[:, cols] + decayed(g, distance.astype(F32)) * arrived(slot, g)

                @pl.when(sends(k))
                def _():
                    total = decayed(g, float(2 * tokens)) * state[:, cols]
                    total = total + decayed(g, float(tokens)) * plocal[:, cols]
                    psend[3, :, cols] = (total + precv[0, :, cols].astype(F32)).astype(BF16)
                    for away in range(1 << k):
                        block_copy(k, g, away).start()

    def sends(k):
        return lax.rem(me, 2 << k) == (1 << k) - 2

    for b in members(0):
        make_tables(b)
    fetches[3].wait()
    fetches[4].wait()

    def after_long(c):
        for g, (_, stop) in enumerate(bounds):
            if stop == c + 1:
                group_done(g)

    for c in range(chunks):
        last = c == chunks - 1
        if last and c > 0:
            long_blocks(members(c - 1))
            after_long(c - 1)

        @pl.when(me > 0)
        def _():
            halo(c).wait_recv()

        short_blocks(members(c))
        if not last:
            for b in members(c + 1):
                make_tables(b)
            if c > 0:
                long_blocks(members(c - 1))
                after_long(c - 1)

    long_blocks(members(chunks - 1))
    after_long(chunks - 1)
    if n <= BLOCK:

        @pl.when(chip < chips - 1)
        def _():
            pl.semaphore_wait(ready, 2 * (chips - 1 - chip))

    even_send_last()
    for g in range(final):
        odd_send(g)
    fetches[5].wait()
    for g in range(final + 1):
        take(g)
        for c in range(*bounds[g]):
            final_blocks(members(c))

    @pl.when(me < n - 1)
    def _():
        halo(0, chunks).wait_send()

    @pl.when(odd == 0)
    def _():
        swap(0, final).wait_send()

    if n > BLOCK:

        @pl.when(jnp.logical_and(odd == 1, chip == chips - 1))
        def _():
            swap(0, final).wait_send()

    @pl.when(jnp.logical_and(odd == 1, chip < chips - 1))
    def _():
        swap(final).wait_send()

    for step in range(1, chips):

        @pl.when(in_later_chip(step))
        def _():
            if final > 0:

                @pl.when(odd == 1)
                def _():
                    chip_copy(0, step, final - 1).wait_send()

            @pl.when(odd == 0)
            def _():
                for core in range(2):
                    last_copy(step, core).wait_send()

    if final > 0:

        @pl.when(jnp.logical_and(odd == 0, chip > 0))
        def _():
            relay(0, final - 1).wait_send()

    for k in range(first_level, levels):

        @pl.when(sends(k))
        def _():
            for away in range(1 << k):
                block_copy(k, 0, away, final).wait_send()


def on_device(n, *args):
    args = args[:6] + (args[6].T, args[7].T)
    args = tuple(pltpu.with_memory_space_constraint(a, pltpu.HBM) for a in args)
    q_short, taps, rates = args[0], args[5], args[6]
    tokens, ch = q_short.shape
    order, groups = rates.shape
    blocks = ch // LANES
    per = LANES * groups // ch
    chunks = max(c for c in (1, 2, 4, 8) if blocks % c == 0)
    levels = n.bit_length() - 1
    chips = min(n, BLOCK) // 2
    above = max(0, levels - chips.bit_length())
    dma = pltpu.SemaphoreType.DMA
    return pl.pallas_call(
        functools.partial(kernel, n, chunks),
        out_shape=jax.ShapeDtypeStruct((tokens, ch), BF16),
        in_specs=[pl.BlockSpec(memory_space=pltpu.HBM)] * 8,
        out_specs=pl.BlockSpec(memory_space=pltpu.VMEM),
        scratch_shapes=[
            pltpu.VMEM((tokens, ch), BF16),
            pltpu.VMEM((tokens, ch), BF16),
            pltpu.VMEM((tokens, ch), BF16),
            pltpu.VMEM((tokens, ch), BF16),
            pltpu.VMEM((tokens, ch), BF16),
            pltpu.VMEM(taps.shape, BF16),
            pltpu.VMEM((order, groups), F32),
            pltpu.VMEM((order, groups), F32),
            dma((6,)),
            dma((2, 2)),
            pltpu.VMEM((blocks, 2 * tokens, LANES), BF16),
            pltpu.VMEM((blocks, tokens, LANES), BF16),
            pltpu.VMEM((blocks, tokens // WINDOWS, WINDOWS * LANES), F32),
            pltpu.VMEM((blocks, 2, per * tokens // SPANS, tokens), BF16),
            pltpu.VMEM((blocks, per // WINDOWS, tokens // WINDOWS + 2 * order, LANES), BF16),
            pltpu.VMEM((blocks, tokens // WINDOWS, LANES), BF16),
            pltpu.VMEM((2, tokens // SPANS, tokens), F32),
            pltpu.VMEM((tokens // WINDOWS, LANES), F32),
            pltpu.VMEM((order, ch), F32),
            pltpu.VMEM((groups, tokens), F32),
            pltpu.VMEM((2, blocks, LANES), F32),
            pltpu.VMEM((2, groups, LANES), F32),
            pltpu.VMEM((order, ch), F32),
            pltpu.VMEM((blocks, order, WINDOWS * LANES), F32),
            pltpu.VMEM((order, ch), F32),
            pltpu.VMEM((4 if above else 3, order, ch), BF16),
            pltpu.VMEM((chips + 1 + above, order, ch), BF16),
            pltpu.SemaphoreType.REGULAR,
            dma,
            dma((chunks,)),
            dma,
            dma((max(1, chips - 1),)),
            dma,
            dma((max(1, chips - 1), 2)),
            dma((max(1, n // 2 if above else 1),)),
            dma((chips + 1 + above, 3)),
        ],
        compiler_params=pltpu.CompilerParams(
            collective_id=0, has_side_effects=True, vmem_limit_bytes=40 * 2**20
        ),
    )(*args)


def solution(mesh):
    in_specs = (P("ctx", "ch"),) * 5 + (P(None, "ch"), P("ch", None), P("ch", None))
    return jax.shard_map(
        functools.partial(on_device, mesh.shape["ctx"]),
        mesh=mesh,
        in_specs=in_specs,
        out_specs=P("ctx", "ch"),
        check_vma=False,
    )
```

time: 16.8 us -> 15.5 us (0.923)
  Pallas kernels: 15.8 us -> 14.4 us
    pallas_call x1, Pallas kernels: 15.8 us -> 14.4 us  [on_device(): pl.pallas_call(functools.partial(kernel, n, chunks), out_shape=jax.ShapeD...]
where the time goes in v3:
time: 15.5 us; the launch traced here: 15.2 us
  Pallas kernels  14.4 us (93%)
  local copies, waits for them, and re-layouts  0.8 us (5%)
    pallas_call x1, Pallas kernels, on_device(): pl.pallas_call(functools.partial(kernel, n, chunks), out_shape=jax.ShapeD...  14.4 us
    unnamed x1, local copies, waits for them, and re-layouts  0.8 us

profile of v3, /device:TPU:29, one launch (start us, length us, event | category | flops | bytes accessed | tf_op | source)
XLA Modules:
  0.0 15.2 jit_solution(4397315669443427964)
XLA Ops:
  0.0 14.4 %shard_map.82 = bf16[128,2048]{1,0:T(8,128)(2,1)S(1)} custom-call(bf16[128,2048]{1,0:T(8,128)(2,1)} %q_short_in.1, bf16[128,2048]{1,0:T(8,128)(2,1)} %k_short_in.1, bf16[128,2048]{1,0:T(8,128)(2,1)} %v_input_in.1, bf16[128,2048]{1,0:T(8,128)(2,1)} %q_long_in.1, bf16[128,2048]{1,0:T(8,128)(2,1)} %k_long_in.1, bf16[128,128]{1,0:T(8,128)(2,1)} %taps_in.1, ...), custom_call_target="tpu_custom_call" | custom-call | tf_op jit(solution)/shard_map/pallas_call | solution.py:501
  14.4 0.8 %copy.10 = bf16[128,2048]{1,0:T(8,128)(2,1)} copy(bf16[128,2048]{1,0:T(8,128)(2,1)S(1)} %shard_map.82) | data formatting | bytes 1048576

commit v4 on v3

--- a/solution.py
+++ b/solution.py
@@ -31,7 +31,7 @@
     n, chunks, q_short_in, k_short_in, v_input_in, q_long_in, k_long_in, taps_in, rates_in, weights_in, out,
     q_short, q_long, k_long, k_short, v_input, taps, rates, weights, fetch_sem, early_sem,
     ubuf, ulong, ynear, short_tab, long_tab, out_tab, masks, long_mask, lam_rc, short_row, modes,
-    turned_modes, state, inner, plocal, psend, precv, ready, halo_send, halo_recv, swap_send, chip_send, relay_send, last_send, block_send, scan_recv,
+    turned_modes, state, inner, plocal, psend, precv, ready, halo_send, halo_recv, swap_send, chip_send, forward_send, merged_send, block_send, scan_recv,
 ):
     me = lax.axis_index("ctx")
     tokens, ch = k_short.shape
@@ -48,7 +48,7 @@
     odd = lax.rem(me, 2)
     chip = lax.rem(me, 2 * chips) // 2
     first_level = (2 * chips).bit_length() - 1
-    bounds = sorted({chunks // 2, chunks - chunks // 4, chunks} - {0})
+    bounds = sorted({chunks // 2, chunks - 1, chunks} - {0})
     bounds = list(zip([0] + bounds[:-1], bounds))
     final = len(bounds) - 1
     parts = 2 if chunks % 2 == 0 else 1
@@ -71,10 +71,6 @@
             )
         )
     ]
-    for part in range(parts):
-        for i in range(2):
-            early(i, part).start()
-
     barrier = pltpu.get_barrier_semaphore()
 
     def signal(semaphore, device):
@@ -83,15 +79,21 @@
         )
 
     if n > BLOCK:
+        for part in range(parts):
+            for i in range(2):
+                early(i, part).start()
         for step in range(1, n):
             signal(barrier, me + step)
     else:
+
+        @pl.when(jnp.logical_and(odd == 0, me > 0))
+        def _():
+            signal(barrier, me - 1)
+
+        for part in range(parts):
+            for i in range(2):
+                early(i, part).start()
         signal(barrier, me + 1 - 2 * odd)
-
-        @pl.when(jnp.logical_and(odd == 0, me > 0))
-        def _():
-            signal(barrier, me - 1)
-
         for step in range(1, chips):
 
             @pl.when(chip + step < chips)
@@ -272,7 +274,7 @@
     def send(source, target, g, send_sem, device, to=None):
         cols = columns(g, to)
         return pltpu.make_async_remote_copy(
-            src_ref=psend.at[source, :, cols],
+            src_ref=source.at[:, cols],
             dst_ref=precv.at[target, :, cols],
             send_sem=send_sem,
             recv_sem=scan_recv.at[target, g],
@@ -281,112 +283,136 @@
         )
 
     def swap(g, to=None):
-        return send(0, 0, g, swap_send, me + 1 - 2 * odd, to)
-
-    def chip_copy(g, step, to=None):
-        return send(1, 1 + chip, g, chip_send.at[step - 1], me + 2 * step - 1, to)
-
-    def relay(g, to=None):
-        return send(2, chips, g, relay_send, me + 1, to)
-
-    def last_copy(step, core):
-        return send(1, 1 + chip, final, last_send.at[step - 1, core], me + 2 * step + core)
+        return send(psend.at[0], 0, g, swap_send, me + 1 - 2 * odd, to)
+
+    def chip_copy(g, step, core, to=None):
+        return send(psend.at[1], 1 + chip, g, chip_send.at[step - 1, core], me - odd + 2 * step + core, to)
+
+    def forward(g, to=None):
+        return send(precv.at[1], 1, g, forward_send, me + 1, to)
+
+    def merged_copy(g, core, to=None):
+        return send(psend.at[2], 2, g, merged_send.at[core], me + 4 + core, to)
 
     def block_copy(k, g, away, to=None):
-        return send(3, chips + 1 + k - first_level, g, block_send.at[away], me + 2 + away, to)
-
-    def arrived(slot, g):
-        send(0, slot, g, swap_send, me + 1).wait_recv()
+        return send(psend.at[3], chips + k - first_level, g, block_send.at[away], me + 2 + away, to)
+
+    def wait_arrival(slot, g):
+        send(psend.at[0], slot, g, swap_send, me + 1).wait_recv()
+
+    def received(slot, g):
         return precv[slot, :, columns(g)].astype(F32)
 
     def decayed(g, distance):
         return jnp.exp2(-lam_rc[:, columns(g)] * distance)
 
-    def in_later_chip(step):
-        return chip + step < chips
+    end_chip = chips - 1
+    inner_chip = jnp.logical_and(chip > 0, chip < end_chip)
+
+    def odd_sends(g):
+        return jnp.logical_and(odd == 1, chip < end_chip if g == 0 else chip == 0)
+
+    def odd_swaps(g):
+        swaps = inner_chip if g > 0 else chip == 1
+        if n > BLOCK:
+            swaps = jnp.logical_or(swaps, chip == end_chip)
+        return jnp.logical_and(odd == 1, swaps)
+
+    def own_total(g):
+        return decayed(g, float(tokens)) * plocal[:, columns(g)] + received(0, g)
 
     def group_done(g):
-        both_ways = jnp.logical_or(odd == 0, chip < chips - 1) if n <= BLOCK else odd >= 0
-        one_way = odd == 0 if n <= BLOCK else jnp.logical_or(odd == 0, chip == chips - 1)
-
-        @pl.when(both_ways if g == final else one_way)
+        @pl.when(jnp.logical_or(odd == 0, odd_swaps(g)))
         def _():
             swap(g).start()
 
+        if g > 0:
+
+            @pl.when(jnp.logical_and(odd == 0, inner_chip))
+            def _():
+                wait_arrival(0, g)
+                psend[1, :, columns(g)] = own_total(g).astype(BF16)
+                for core in range(2):
+                    chip_copy(g, 1, core).start()
+
     def odd_send(g):
-        @pl.when(jnp.logical_and(odd == 1, chip < chips - 1))
-        def _():
-            total = decayed(g, float(tokens)) * arrived(0, g) + plocal[:, columns(g)]
+        @pl.when(odd_sends(g))
+        def _():
+            wait_arrival(0, g)
+            total = decayed(g, float(tokens)) * received(0, g) + plocal[:, columns(g)]
             psend[1, :, columns(g)] = total.astype(BF16)
-            for step in range(1, chips):
-
-                @pl.when(in_later_chip(step))
+            chip_copy(g, 1, 0).start()
+
+            @pl.when(chip == 0)
+            def _():
+                chip_copy(g, 2, 0).start()
+
+            if g == 0:
+
+                @pl.when(chip > 0)
                 def _():
-                    chip_copy(g, step).start()
-
-    def even_send_last():
-        @pl.when(jnp.logical_and(odd == 0, chip < chips - 1))
-        def _():
-            total = decayed(final, float(tokens)) * plocal[:, columns(final)] + arrived(0, final)
-            psend[1, :, columns(final)] = total.astype(BF16)
-            for step in range(1, chips):
-
-                @pl.when(in_later_chip(step))
-                def _():
-                    for core in range(2):
-                        last_copy(step, core).start()
-
-    def take_chips(g, cores):
+                    chip_copy(g, 1, 1).start()
+
+    def pass_first(g):
+        @pl.when(jnp.logical_and(odd == 0, inner_chip))
+        def _():
+            wait_arrival(1, g)
+
+        @pl.when(jnp.logical_and(odd == 0, chip == 1))
+        def _():
+            if g == 0:
+                wait_arrival(0, g)
+            total = decayed(g, float(2 * tokens)) * received(1, g) + own_total(g)
+            psend[2, :, columns(g)] = total.astype(BF16)
+            for core in range(2):
+                merged_copy(g, core).start()
+
+        @pl.when(jnp.logical_and(odd == 0, inner_chip))
+        def _():
+            forward(g).start()
+
+    def take(g):
         cols = columns(g)
         for source in range(chips - 1):
-
-            @pl.when(jnp.logical_and(chip > source, odd < cores))
+            reached = inner_chip if source == 0 else chip > source
+
+            @pl.when(jnp.logical_and(reached, odd == 1) if source == 0 else reached)
+            def _():
+                wait_arrival(1 + source, g)
+
+            @pl.when(reached)
             def _():
                 distance = ((chip - source - 1) * 2 + odd) * tokens
-                state[:, cols] = state[:, cols] + decayed(g, distance.astype(F32)) * arrived(1 + source, g)
-
-    def take(g):
-        cols = columns(g)
-        take_chips(g, 1 if g < final else 2)
-        if g < final:
-
-            @pl.when(jnp.logical_and(odd == 0, chip > 0))
-            def _():
-                psend[2, :, cols] = state[:, cols].astype(BF16)
-                relay(g).start()
-
-            @pl.when(jnp.logical_and(odd == 1, chip > 0))
-            def _():
-                state[:, cols] = decayed(g, float(tokens)) * arrived(chips, g)
-
-        @pl.when(jnp.logical_and(odd == 1, jnp.logical_or(chip == chips - 1, g == final)))
-        def _():
-            send(0, 0, g, swap_send, me + 1).wait_recv()
+                state[:, cols] = state[:, cols] + decayed(g, distance.astype(F32)) * received(1 + source, g)
+
+        @pl.when(jnp.logical_and(odd == 1, jnp.logical_not(odd_sends(g))))
+        def _():
+            wait_arrival(0, g)
 
         @pl.when(odd == 1)
         def _():
-            state[:, cols] = state[:, cols] + precv[0, :, cols].astype(F32)
+            state[:, cols] = state[:, cols] + received(0, g)
 
         if n > BLOCK:
-            last_even = jnp.logical_and(odd == 0, chip == chips - 1)
-
-            @pl.when(last_even)
-            def _():
-                send(0, 0, g, swap_send, me + 1).wait_recv()
+
+            @pl.when(jnp.logical_and(odd == 0, chip == end_chip))
+            def _():
+                wait_arrival(0, g)
 
             for k in range(first_level, levels):
 
                 @pl.when(lax.rem(me, 2 << k) >= 1 << k)
                 def _():
                     distance = lax.rem(me, 1 << k) * tokens
-                    slot = chips + 1 + k - first_level
-                    state[:, cols] = state[:, cols] + decayed(g, distance.astype(F32)) * arrived(slot, g)
+                    slot = chips + k - first_level
+                    wait_arrival(slot, g)
+                    state[:, cols] = state[:, cols] + decayed(g, distance.astype(F32)) * received(slot, g)
 
                 @pl.when(sends(k))
                 def _():
                     total = decayed(g, float(2 * tokens)) * state[:, cols]
                     total = total + decayed(g, float(tokens)) * plocal[:, cols]
-                    psend[3, :, cols] = (total + precv[0, :, cols].astype(F32)).astype(BF16)
+                    psend[3, :, cols] = (total + received(0, g)).astype(BF16)
                     for away in range(1 << k):
                         block_copy(k, g, away).start()
 
@@ -405,6 +431,12 @@
 
     for c in range(chunks):
         last = c == chunks - 1
+        if c == chunks // 2 and n <= BLOCK:
+
+            @pl.when(chip < chips - 1)
+            def _():
+                pl.semaphore_wait(ready, 2 * (chips - 1 - chip))
+
         if last and c > 0:
             long_blocks(members(c - 1))
             after_long(c - 1)
@@ -423,15 +455,10 @@
 
     long_blocks(members(chunks - 1))
     after_long(chunks - 1)
-    if n <= BLOCK:
-
-        @pl.when(chip < chips - 1)
-        def _():
-            pl.semaphore_wait(ready, 2 * (chips - 1 - chip))
-
-    even_send_last()
-    for g in range(final):
+    for g in range(final + 1):
         odd_send(g)
+    for g in range(final + 1):
+        pass_first(g)
     fetches[5].wait()
     for g in range(final + 1):
         take(g)
@@ -448,34 +475,41 @@
 
     if n > BLOCK:
 
-        @pl.when(jnp.logical_and(odd == 1, chip == chips - 1))
+        @pl.when(jnp.logical_and(odd == 1, chip == end_chip))
         def _():
             swap(0, final).wait_send()
 
-    @pl.when(jnp.logical_and(odd == 1, chip < chips - 1))
+    for place, first in ((1, 0), (2, 1)):
+
+        @pl.when(jnp.logical_and(odd == 1, chip == place))
+        def _():
+            swap(first, final).wait_send()
+
+    @pl.when(jnp.logical_and(odd == 1, chip == 0))
     def _():
-        swap(final).wait_send()
-
-    for step in range(1, chips):
-
-        @pl.when(in_later_chip(step))
-        def _():
-            if final > 0:
-
-                @pl.when(odd == 1)
-                def _():
-                    chip_copy(0, step, final - 1).wait_send()
+        for step in range(1, 3):
+            chip_copy(0, step, 0, final).wait_send()
+
+    @pl.when(inner_chip)
+    def _():
+        for core in range(2):
+
+            @pl.when(odd == 1)
+            def _():
+                chip_copy(0, 1, core).wait_send()
 
             @pl.when(odd == 0)
             def _():
-                for core in range(2):
-                    last_copy(step, core).wait_send()
-
-    if final > 0:
-
-        @pl.when(jnp.logical_and(odd == 0, chip > 0))
-        def _():
-            relay(0, final - 1).wait_send()
+                chip_copy(1, 1, core, final).wait_send()
+
+        @pl.when(odd == 0)
+        def _():
+            forward(0, final).wait_send()
+
+    @pl.when(jnp.logical_and(odd == 0, chip == 1))
+    def _():
+        for core in range(2):
+            merged_copy(0, core, final).wait_send()
 
     for k in range(first_level, levels):
 
@@ -530,16 +564,16 @@
             pltpu.VMEM((blocks, order, WINDOWS * LANES), F32),
             pltpu.VMEM((order, ch), F32),
             pltpu.VMEM((4 if above else 3, order, ch), BF16),
-            pltpu.VMEM((chips + 1 + above, order, ch), BF16),
+            pltpu.VMEM((chips + above, order, ch), BF16),
             pltpu.SemaphoreType.REGULAR,
             dma,
             dma((chunks,)),
             dma,
-            dma((max(1, chips - 1),)),
+            dma((2, 2)),
             dma,
-            dma((max(1, chips - 1), 2)),
+            dma((2,)),
             dma((max(1, n // 2 if above else 1),)),
-            dma((chips + 1 + above, 3)),
+            dma((chips + above, 3)),
         ],
         compiler_params=pltpu.CompilerParams(
             collective_id=0, has_side_effects=True, vmem_limit_bytes=40 * 2**20

time: 15.5 us -> 14.5 us (0.935)
  the two profiles are of different devices: /device:TPU:29 before, /device:TPU:7 now
where the time goes in v4:
time: 14.5 us; the launch traced here: 14.4 us
  Pallas kernels  13.6 us (94%)
  local copies, waits for them, and re-layouts  0.8 us (6%)
    pallas_call x1, Pallas kernels, on_device(): pl.pallas_call(functools.partial(kernel, n, chunks), out_shape=jax.ShapeD...  13.6 us
    unnamed x1, local copies, waits for them, and re-layouts  0.8 us

profile of v4, /device:TPU:7, one launch (start us, length us, event | category | flops | bytes accessed | tf_op | source)
XLA Modules:
  0.0 14.4 jit_solution(8278459263833173757)
XLA Ops:
  0.0 13.6 %shard_map.82 = bf16[128,2048]{1,0:T(8,128)(2,1)S(1)} custom-call(bf16[128,2048]{1,0:T(8,128)(2,1)} %q_short_in.1, bf16[128,2048]{1,0:T(8,128)(2,1)} %k_short_in.1, bf16[128,2048]{1,0:T(8,128)(2,1)} %v_input_in.1, bf16[128,2048]{1,0:T(8,128)(2,1)} %q_long_in.1, bf16[128,2048]{1,0:T(8,128)(2,1)} %k_long_in.1, bf16[128,128]{1,0:T(8,128)(2,1)} %taps_in.1, ...), custom_call_target="tpu_custom_call" | custom-call | tf_op jit(solution)/shard_map/pallas_call | solution.py:535
  13.6 0.8 %copy.10 = bf16[128,2048]{1,0:T(8,128)(2,1)} copy(bf16[128,2048]{1,0:T(8,128)(2,1)S(1)} %shard_map.82) | data formatting | bytes 1048576

commit v5 on v4

--- a/solution.py
+++ b/solution.py
@@ -165,7 +165,7 @@
     ahead = (lax.rem(lane, size) - size).astype(F32)
     first = lax.rem(lane, size) == 0
     first_row = lax.rem(iota((1, LANES), 1), size) == 0
-    rows = -iota((size, LANES), 0).astype(F32)
+    rows = -iota((tokens, LANES), 0).astype(F32)
     masks[0] = (iota((tap_rows, tokens), 0) < iota((tap_rows, tokens), 1)).astype(F32)
     masks[1] = (iota((tap_rows, tokens), 0) >= iota((tap_rows, tokens), 1)).astype(F32)
     long_mask[...] = (iota((size, LANES), 0) >= lax.rem(iota((size, LANES), 1), size)).astype(F32)
@@ -244,24 +244,36 @@
             plocal[:, cols] = total
             psend[0, :, cols] = total.astype(BF16)
 
+    def expanded(x):
+        group = lane_group_order[:, : x.shape[1]]
+        return jnp.concatenate(
+            [jnp.where(group == g, part, jnp.zeros_like(part)) for part in split(x) for g in range(per)], 0
+        )
+
+    def inner_blocks(bs):
+        for b in bs:
+            cols = pl.ds(b * LANES, LANES)
+            decay = jnp.exp2(-lam_rc[:, cols] * float(size))
+            sums = pieces(inner[b])[:-1]
+            starts = [sums[0]]
+            for piece in sums[1:]:
+                starts.append(decay * starts[-1] + piece)
+            table = out_tab[b, pl.ds(0, size), :]
+            far = jnp.dot(
+                jnp.concatenate([table, table], 1),
+                expanded(jnp.concatenate(starts, 1)),
+                preferred_element_type=F32,
+            )
+            ynear[b, :, pl.ds(LANES, (WINDOWS - 1) * LANES)] += far
+
     def final_blocks(bs):
         for b in bs:
             cols = pl.ds(b * LANES, LANES)
-            decay = jnp.exp2(-lam_rc[:, cols] * float(size))
-            starts = [state[:, cols]]
-            for piece in pieces(inner[b])[:-1]:
-                starts.append(decay * starts[-1] + piece)
-            tall = jnp.concatenate(
-                [
-                    jnp.where(lane_group_order == g, x, jnp.zeros_like(x))
-                    for x in split(jnp.concatenate(starts, 1))
-                    for g in range(per)
-                ],
-                0,
+            table = out_tab[b]
+            far = jnp.dot(
+                jnp.concatenate([table, table], 1), expanded(state[:, cols]), preferred_element_type=F32
             )
-            table = out_tab[b]
-            far = jnp.dot(jnp.concatenate([table, table], 1), tall, preferred_element_type=F32)
-            y = stacked(ynear[b] + far).astype(BF16)
+            y = (stacked(ynear[b]) + far).astype(BF16)
             out[:, cols] = (q_long[:, cols].astype(F32) * y.astype(F32)).astype(BF16)
 
     def members(c):
@@ -364,7 +376,7 @@
                 wait_arrival(0, g)
             total = decayed(g, float(2 * tokens)) * received(1, g) + own_total(g)
             psend[2, :, columns(g)] = total.astype(BF16)
-            for core in range(2):
+            for core in (1, 0):
                 merged_copy(g, core).start()
 
         @pl.when(jnp.logical_and(odd == 0, inner_chip))
@@ -440,6 +452,8 @@
         if last and c > 0:
             long_blocks(members(c - 1))
             after_long(c - 1)
+            if c > 1:
+                inner_blocks(members(c - 2))
 
         @pl.when(me > 0)
         def _():
@@ -451,6 +465,8 @@
                 make_tables(b)
             if c > 0:
                 long_blocks(members(c - 1))
+                if c > 1:
+                    inner_blocks(members(c - 2))
                 after_long(c - 1)
 
     long_blocks(members(chunks - 1))
@@ -459,6 +475,8 @@
         odd_send(g)
     for g in range(final + 1):
         pass_first(g)
+    for c in range(max(0, chunks - 2), chunks):
+        inner_blocks(members(c))
     fetches[5].wait()
     for g in range(final + 1):
         take(g)
@@ -553,7 +571,7 @@
             pltpu.VMEM((blocks, tokens // WINDOWS, WINDOWS * LANES), F32),
             pltpu.VMEM((blocks, 2, per * tokens // SPANS, tokens), BF16),
             pltpu.VMEM((blocks, per // WINDOWS, tokens // WINDOWS + 2 * order, LANES), BF16),
-            pltpu.VMEM((blocks, tokens // WINDOWS, LANES), BF16),
+            pltpu.VMEM((blocks, tokens, LANES), BF16),
             pltpu.VMEM((2, tokens // SPANS, tokens), F32),
             pltpu.VMEM((tokens // WINDOWS, LANES), F32),
             pltpu.VMEM((order, ch), F32),

time: 14.5 us -> 14.3 us (0.986)
  the two profiles are of different devices: /device:TPU:7 before, /device:TPU:30 now
where the time goes in v5:
time: 14.3 us; the launch traced here: 14.1 us
  Pallas kernels  13.3 us (93%)
  local copies, waits for them, and re-layouts  0.8 us (6%)
    pallas_call x1, Pallas kernels, on_device(): pl.pallas_call(functools.partial(kernel, n, chunks), out_shape=jax.ShapeD...  13.3 us
    unnamed x1, local copies, waits for them, and re-layouts  0.8 us

profile of v5, /device:TPU:30, one launch (start us, length us, event | category | flops | bytes accessed | tf_op | source)
XLA Modules:
  0.0 14.1 jit_solution(15316657460952989765)
XLA Ops:
  0.0 13.3 %shard_map.82 = bf16[128,2048]{1,0:T(8,128)(2,1)S(1)} custom-call(bf16[128,2048]{1,0:T(8,128)(2,1)} %q_short_in.1, bf16[128,2048]{1,0:T(8,128)(2,1)} %k_short_in.1, bf16[128,2048]{1,0:T(8,128)(2,1)} %v_input_in.1, bf16[128,2048]{1,0:T(8,128)(2,1)} %q_long_in.1, bf16[128,2048]{1,0:T(8,128)(2,1)} %k_long_in.1, bf16[128,128]{1,0:T(8,128)(2,1)} %taps_in.1, ...), custom_call_target="tpu_custom_call" | custom-call | tf_op jit(solution)/shard_map/pallas_call | solution.py:553
  13.3 0.8 %copy.10 = bf16[128,2048]{1,0:T(8,128)(2,1)} copy(bf16[128,2048]{1,0:T(8,128)(2,1)S(1)} %shard_map.82) | data formatting | bytes 1048576

commit v6 on v5

--- a/solution.py
+++ b/solution.py
@@ -365,19 +365,21 @@
                 def _():
                     chip_copy(g, 1, 1).start()
 
-    def pass_first(g):
-        @pl.when(jnp.logical_and(odd == 0, inner_chip))
+    def merge(g):
+        @pl.when(jnp.logical_and(odd == 0, chip == 1))
         def _():
             wait_arrival(1, g)
-
-        @pl.when(jnp.logical_and(odd == 0, chip == 1))
-        def _():
             if g == 0:
                 wait_arrival(0, g)
             total = decayed(g, float(2 * tokens)) * received(1, g) + own_total(g)
             psend[2, :, columns(g)] = total.astype(BF16)
             for core in (1, 0):
                 merged_copy(g, core).start()
+
+    def pass_first(g):
+        @pl.when(jnp.logical_and(odd == 0, chip == 2))
+        def _():
+            wait_arrival(1, g)
 
         @pl.when(jnp.logical_and(odd == 0, inner_chip))
         def _():
@@ -431,8 +433,10 @@
     def sends(k):
         return lax.rem(me, 2 << k) == (1 << k) - 2
 
-    for b in members(0):
-        make_tables(b)
+    lead = max(1, chunks // 2)
+    for c in range(lead):
+        for b in members(c):
+            make_tables(b)
     fetches[3].wait()
     fetches[4].wait()
 
@@ -452,8 +456,6 @@
         if last and c > 0:
             long_blocks(members(c - 1))
             after_long(c - 1)
-            if c > 1:
-                inner_blocks(members(c - 2))
 
         @pl.when(me > 0)
         def _():
@@ -461,21 +463,25 @@
 
         short_blocks(members(c))
         if not last:
-            for b in members(c + 1):
-                make_tables(b)
+            if c + lead < chunks:
+                for b in members(c + lead):
+                    make_tables(b)
             if c > 0:
                 long_blocks(members(c - 1))
-                if c > 1:
+                if 1 < c < chunks - 2:
                     inner_blocks(members(c - 2))
                 after_long(c - 1)
 
+    merge(0)
     long_blocks(members(chunks - 1))
     after_long(chunks - 1)
     for g in range(final + 1):
         odd_send(g)
+    for g in range(1, final + 1):
+        merge(g)
     for g in range(final + 1):
         pass_first(g)
-    for c in range(max(0, chunks - 2), chunks):
+    for c in range(max(0, chunks - 4), chunks):
         inner_blocks(members(c))
     fetches[5].wait()
     for g in range(final + 1):

time: 14.3 us -> 14.2 us (level)
  the two profiles are of different devices: /device:TPU:30 before, /device:TPU:29 now
where the time goes in v6:
time: 14.2 us; the launch traced here: 14 us
  Pallas kernels  13.2 us (93%)
  local copies, waits for them, and re-layouts  0.8 us (6%)
    pallas_call x1, Pallas kernels, on_device(): pl.pallas_call(functools.partial(kernel, n, chunks), out_shape=jax.ShapeD...  13.2 us
    unnamed x1, local copies, waits for them, and re-layouts  0.8 us

profile of v6, /device:TPU:29, one launch (start us, length us, event | category | flops | bytes accessed | tf_op | source)
XLA Modules:
  0.0 14.0 jit_solution(18145930854145191261)
XLA Ops:
  0.0 13.2 %shard_map.82 = bf16[128,2048]{1,0:T(8,128)(2,1)S(1)} custom-call(bf16[128,2048]{1,0:T(8,128)(2,1)} %q_short_in.1, bf16[128,2048]{1,0:T(8,128)(2,1)} %k_short_in.1, bf16[128,2048]{1,0:T(8,128)(2,1)} %v_input_in.1, bf16[128,2048]{1,0:T(8,128)(2,1)} %q_long_in.1, bf16[128,2048]{1,0:T(8,128)(2,1)} %k_long_in.1, bf16[128,128]{1,0:T(8,128)(2,1)} %taps_in.1, ...), custom_call_target="tpu_custom_call" | custom-call | tf_op jit(solution)/shard_map/pallas_call | solution.py:559
  13.2 0.8 %copy.10 = bf16[128,2048]{1,0:T(8,128)(2,1)} copy(bf16[128,2048]{1,0:T(8,128)(2,1)S(1)} %shard_map.82) | data formatting | bytes 1048576

commit v7 on v6

--- a/solution.py
+++ b/solution.py
@@ -433,7 +433,7 @@
     def sends(k):
         return lax.rem(me, 2 << k) == (1 << k) - 2
 
-    lead = max(1, chunks // 2)
+    lead = max(1, chunks // 4)
     for c in range(lead):
         for b in members(c):
             make_tables(b)

time: 14.2 us -> 14.2 us (level)
  no operation moved by 1% of the time
where the time goes in v7:
time: 14.2 us; the launch traced here: 14 us
  Pallas kernels  13.2 us (93%)
  local copies, waits for them, and re-layouts  0.8 us (6%)
    pallas_call x1, Pallas kernels, on_device(): pl.pallas_call(functools.partial(kernel, n, chunks), out_shape=jax.ShapeD...  13.2 us
    unnamed x1, local copies, waits for them, and re-layouts  0.8 us

profile of v7, /device:TPU:29, one launch (start us, length us, event | category | flops | bytes accessed | tf_op | source)
XLA Modules:
  0.0 14.0 jit_solution(15909951796458490108)
XLA Ops:
  0.0 13.2 %shard_map.82 = bf16[128,2048]{1,0:T(8,128)(2,1)S(1)} custom-call(bf16[128,2048]{1,0:T(8,128)(2,1)} %q_short_in.1, bf16[128,2048]{1,0:T(8,128)(2,1)} %k_short_in.1, bf16[128,2048]{1,0:T(8,128)(2,1)} %v_input_in.1, bf16[128,2048]{1,0:T(8,128)(2,1)} %q_long_in.1, bf16[128,2048]{1,0:T(8,128)(2,1)} %k_long_in.1, bf16[128,128]{1,0:T(8,128)(2,1)} %taps_in.1, ...), custom_call_target="tpu_custom_call" | custom-call | tf_op jit(solution)/shard_map/pallas_call | solution.py:559
  13.2 0.8 %copy.10 = bf16[128,2048]{1,0:T(8,128)(2,1)} copy(bf16[128,2048]{1,0:T(8,128)(2,1)S(1)} %shard_map.82) | data formatting | bytes 1048576
